TPU v7x, 512 devices: a whole 4x4x16 slice. The times are simulated.
512 devices in a mesh: inb: 16 (over y, z_lo), hid: 32 (over z_hi, x, core).
Axes of the slice: x: 4, y: 4, z: 16 (z_hi: 4, z_lo: 4; z = z_hi * 4 + z_lo), core: 2. Of those that a mesh axis runs over, the one named last changes fastest.
Arguments:
- activations: bfloat16 [2, 512, 16384], P(None, 'hid', 'inb'), may hold values from -40 to 40
- out_grads: bfloat16 [2, 512, 32768], P(None, 'inb', 'hid'), may hold values from -1 to 1
- basis_in: bfloat16 [16384, 1024], P('inb', 'hid'), may hold values from -0.1875 to 0.1875
- basis_out: bfloat16 [32768, 1024], P('hid', 'inb'), may hold values from -0.1875 to 0.1875
Outputs:
- precond: bfloat16 [16384, 32768], P('inb', 'hid')
All inputs are finite; a program needn't handle non-finite values.
Results may differ from a plain program's by a relative error of at most 0.0058.
Values may be sent and summed in bfloat16 or wider, within the bound.
A program may use at most 64 MiB of HBM per device.

v0:
```python
import jax
import jax.numpy as jnp
from jax import lax
from jax.sharding import PartitionSpec as P

damping = 0.1


def square_round(values):
    widened = values.astype(jnp.float32)
    return (widened * widened).astype(jnp.bfloat16)


def contract_tokens(left_side, right_side):
    return lax.dot_general(
        left_side, right_side, (((0, 1), (0, 1)), ((), ())), preferred_element_type=jnp.float32
    )


def on_device(activations, out_grads, basis_in, basis_out):
    micro_count = activations.shape[0]
    width_block = basis_in.shape[0]
    grads_flat = out_grads.reshape(-1, width_block)
    grads_rot = (
        jnp.dot(
            grads_flat,
            lax.all_gather(basis_out, "inb", axis=1, tiled=True),
            preferred_element_type=jnp.float32,
        )
        .astype(jnp.bfloat16)
        .reshape(out_grads.shape)
    )
    basis_whole = lax.all_gather(basis_in, "hid", axis=1, tiled=True)
    groups = [(number, number + 1) for number in range(micro_count)]
    grad_sum = jnp.zeros((width_block, width_block), jnp.float32)
    fisher_sum = jnp.zeros((width_block, width_block), jnp.float32)
    for lower_mb, upper_mb in groups:
        grads_full = lax.all_gather(grads_rot[lower_mb:upper_mb], "inb", axis=1, tiled=True)
        grads_squared = square_round(grads_full)
        plain_rows = lax.all_gather(activations[lower_mb:upper_mb], "hid", axis=1, tiled=True)
        rotated = (
            jnp.dot(
                plain_rows.reshape(-1, width_block), basis_whole, preferred_element_type=jnp.float32
            )
            .astype(jnp.bfloat16)
            .reshape(plain_rows.shape)
        )
        grad_sum = grad_sum + contract_tokens(rotated, grads_full)
        fisher_sum = fisher_sum + contract_tokens(square_round(rotated), grads_squared)
    return (grad_sum / (fisher_sum + damping)).astype(jnp.bfloat16)


def solution(mesh):
    return jax.shard_map(
        on_device,
        mesh=mesh,
        in_specs=(P(None, "hid", "inb"), P(None, "inb", "hid"), P("inb", "hid"), P("hid", "inb")),
        out_specs=P("inb", "hid"),
        check_vma=False,
    )
```

profile of v0, /device:TPU:1, one launch (start us, length us, event | category | flops | bytes accessed | tf_op | source)
XLA Modules:
  0.0 500.0 jit_solution(13084223138114623987)
XLA Ops:
  6.5 0.0 copy-start
  6.5 0.0 all-gather.13.cloned.1.call-start
  6.5 0.7 all-gather.13.cloned.1.call-update
  7.3 0.0 all-gather.15.cloned.1.call-start
  7.3 1.4 fusion.4
  8.7 0.0 all-gather.15.cloned.1.call-update
  8.7 0.0 all-gather.11.cloned.1.call-start
  8.8 0.7 all-gather.11.cloned.1.call-update
  9.5 0.0 all-gather.9.cloned.1.call-start
  9.5 0.5 all-gather.9.cloned.1.call-update
  10.0 0.0 all-gather.17.cloned.1.call-start
  10.1 87.3 %all-gather.13.cloned.1.call-done = bf16[1024,1024]{0,1:T(8,128)(2,1)} async-done(((bf16[1024,64]{0,1:T(8,128)(2,1)}), bf16[1024,1024]{0,1:T(8,128)(2,1)}) %all-gather.13.cloned.1.call-update) | async-done | bytes 2097168 | tf_op jit(solution)/shard_map/all_gather | solution.py:27
  97.4 0.0 copy-done
  97.4 2.3 convolution_convert_fusion.2
  99.8 0.7 fusion.3
  100.4 0.0 all-gather.17.cloned.1.call-update
  100.5 0.0 all-gather.19.cloned.1.call-start
  100.5 0.5 all-gather.19.cloned.1.call-update
  101.0 79.8 %all-gather.15.cloned.1.call-done = bf16[1,512,1024]{2,1,0:T(8,128)(2,1)} async-done(((bf16[1,16,1024]{2,1,0:T(8,128)(2,1)}), bf16[1,512,1024]{2,1,0:T(8,128)(2,1)}) %all-gather.15.cloned.1.call-update) | async-done | bytes 1048592 | tf_op jit(solution)/shard_map/all_gather | solution.py:40
  180.8 75.6 %all-gather.11.cloned.1.call-done = bf16[1024,1024]{0,1:T(8,128)(2,1)} async-done(((bf16[1024,32]{0,1:T(8,128)(2,1)}), bf16[1024,1024]{0,1:T(8,128)(2,1)}) %all-gather.11.cloned.1.call-update) | async-done | bytes 2097168 | tf_op jit(solution)/shard_map/all_gather | solution.py:33
  256.4 3.2 convolution_convert_fusion
  259.6 65.7 %all-gather.9.cloned.1.call-done = bf16[1,512,1024]{2,1,0:T(8,128)(2,1)} async-done(((bf16[1,16,1024]{2,1,0:T(8,128)(2,1)}), bf16[1,512,1024]{2,1,0:T(8,128)(2,1)}) %all-gather.9.cloned.1.call-update) | async-done | bytes 1048592 | tf_op jit(solution)/shard_map/all_gather | solution.py:40
  325.4 3.2 convolution_convert_fusion.1
  328.6 68.7 %all-gather.17.cloned.1.call-done = bf16[512,1024]{1,0:T(8,128)(2,1)} async-done(((bf16[32,1024]{1,0:T(8,128)(2,1)}), bf16[512,1024]{1,0:T(8,128)(2,1)}) %all-gather.17.cloned.1.call-update) | async-done | bytes 1048592 | tf_op jit(solution)/shard_map/all_gather | solution.py:38
  397.2 0.0 copy-start.2
  397.2 4.5 fusion
  401.8 0.0 copy-done.2
  401.8 3.3 fusion.5
  405.1 79.8 %all-gather.19.cloned.1.call-done = bf16[512,1024]{1,0:T(8,128)(2,1)} async-done(((bf16[32,1024]{1,0:T(8,128)(2,1)}), bf16[512,1024]{1,0:T(8,128)(2,1)}) %all-gather.19.cloned.1.call-update) | async-done | bytes 1048592 | tf_op jit(solution)/shard_map/all_gather | solution.py:38
  484.9 0.0 copy-start.1
  484.9 0.0 copy-start.3
  484.9 2.7 fusion.6
  487.5 0.0 copy-done.1
  487.6 0.1 copy-done.3
  487.7 5.5 %divide_convert_fusion = bf16[1024,1024]{1,0:T(8,128)(2,1)} fusion(f32[1024,1024]{1,0:T(8,128)} %fusion, f32[1024,1024]{1,0:T(8,128)S(1)} %copy-done.1, f32[1024,1024]{1,0:T(8,128)S(1)} %fusion.6, bf16[512,1024]{1,0:T(8,128)(2,1)S(1)} %convolution_convert_fusion, bf16[512,1024]{1,0:T(8,128)(2,1)S(1)} %copy-done.3), kind=kOutput, calls=%fused_computation | convolution fusion | flops 1082130432 | bytes 16777216 | tf_op jit(solution)/shard_map/dot_general | solution.py:15
Async XLA Ops:
  6.5 90.9 %copy-start = (bf16[2,32,1024]{2,1,0:T(8,128)(2,1)S(1)}, bf16[2,32,1024]{2,1,0:T(8,128)(2,1)}, u32[]{:S(2)}) copy-start(bf16[2,32,1024]{2,1,0:T(8,128)(2,1)} %param.5) | copy-start | bytes 393220
  6.5 90.9 %all-gather.13.cloned.1.call-start = ((), (), s32[]{:S(2)}) async-start(), calls=%async_computation.2 | async-start | bytes 2228224 | tf_op jit(solution)/shard_map/all_gather | solution.py:27
  7.3 173.6 %all-gather.15.cloned.1.call-start = ((), (), s32[]{:S(2)}) async-start(), calls=%async_computation.3 | async-start | bytes 1081344 | tf_op jit(solution)/shard_map/all_gather | solution.py:40
  8.7 247.7 %all-gather.11.cloned.1.call-start = ((), (), s32[]{:S(2)}) async-start(), calls=%async_computation.1 | async-start | bytes 2162688 | tf_op jit(solution)/shard_map/all_gather | solution.py:33
  9.5 315.9 %all-gather.9.cloned.1.call-start = ((), (), s32[]{:S(2)}) async-start(), calls=%async_computation | async-start | bytes 1081344 | tf_op jit(solution)/shard_map/all_gather | solution.py:40
  10.0 387.2 %all-gather.17.cloned.1.call-start = ((), (), s32[]{:S(2)}) async-start(), calls=%async_computation.4 | async-start | bytes 1114112 | tf_op jit(solution)/shard_map/all_gather | solution.py:38
  100.5 384.4 %all-gather.19.cloned.1.call-start = ((), (), s32[]{:S(2)}) async-start(), calls=%async_computation.5 | async-start | bytes 1114112 | tf_op jit(solution)/shard_map/all_gather | solution.py:38
  397.2 4.6 copy-start.2
  484.9 2.7 copy-start.1
  484.9 2.8 copy-start.3
Sparse Core Ops, SparseCore 0:
  9.4 87.9 all-gather.12
  100.6 80.2 all-gather.14
  184.0 72.4 all-gather.10
  259.4 65.8 all-gather.8
  327.3 69.8 all-gather.16
  399.2 85.6 all-gather.18
where the time goes:
time: 510 us; the launch traced here: 500 us
  waiting for transfers between devices  459 us (90%)
  matrix products  24.8 us (5%)
  between operations  13.5 us (3%)
    all_gather x2, waiting for transfers between devices, on_device(): lax.all_gather(grads_rot[lower_mb:upper_mb], 'inb', axis=1, tiled=True)  148 us
    all_gather x2, waiting for transfers between devices, on_device(): lax.all_gather(activations[lower_mb:upper_mb], 'hid', axis=1, tiled=True)  146 us
    all_gather x1, waiting for transfers between devices, on_device(): lax.all_gather(basis_out, 'inb', axis=1, tiled=True)  87.3 us
    all_gather x1, waiting for transfers between devices, on_device(): basis_whole = lax.all_gather(basis_in, 'hid', axis=1, tiled=True)  75.6 us
    dot_general x4, matrix products, contract_tokens(): lax.dot_general(left_side, right_side, (((0, 1), (0, 1)), ((), ())), pref...  16 us
  transfers between devices with their start and end apart: 6, of which 6 were waited for; matrix products, arithmetic and copies ran while one was open for 4% of the time, Pallas kernels for 0%

commit v1 on v0

v1 whole, which is shorter than its diff:
```python
import functools

import jax
import jax.numpy as jnp
from jax import lax
from jax.experimental import pallas as pl
from jax.experimental.pallas import tpu as pltpu
from jax.sharding import PartitionSpec as P

damping = 0.1
MESH = pl.DeviceIdType.MESH
bf16 = jnp.bfloat16
f32 = jnp.float32


class Names:
    def __init__(self):
        self.slots = {}

    def __getitem__(self, name):
        return self.slots.setdefault(name, len(self.slots))


def square(values):
    wide = values.astype(f32)
    return (wide * wide).astype(bf16)


def nt_dot(left, right):
    return lax.dot_general(
        left, right, (((1,), (1,)), ((), ())), preferred_element_type=f32
    )


def kernel(
    acts, grads, bin_t, bout_t, out,
    TB, CB, RO, SO, TH, CH, RT, ST, load_sem, send_sem, recv_sem,
):
    inb = lax.axis_index("inb")
    hid = lax.axis_index("hid")
    y, zl = inb // 4, inb % 4
    zh, x, c = hid // 8, (hid // 2) % 4, hid % 2
    Y1, Y0, Z1, Z0 = y // 2, y % 2, zl // 2, zl % 2
    is_mid = (zl == 1) | (zl == 2)

    def flip(value, mask):
        for bit in (1, 2):
            if mask & bit:
                value = value + bit - 2 * bit * ((value // bit) % 2)
        return value

    def peer(dy=0, dzl=0, dzh=0, dx=0, dc=0):
        return (
            flip(y, dy) * 4 + flip(zl, dzl),
            flip(zh, dzh) * 8 + flip(x, dx) * 2 + flip(c, dc),
        )

    def xx(position):
        return (position % 2) * 2 + position // 2

    slots, sends = Names(), []

    def send(name, ref, whom, when=None):
        slot = slots[name]
        copy = pltpu.make_async_remote_copy(
            ref, ref, send_sem.at[len(sends)], recv_sem.at[slot],
            device_id=whom, device_id_type=MESH,
        )
        sends.append((copy, when))
        if when is None:
            copy.start()
        else:
            pl.when(when)(copy.start)

    def send_to(name, ref, target, whom):
        copy = pltpu.make_async_remote_copy(
            ref, target, send_sem.at[len(sends)], recv_sem.at[slots[name]],
            device_id=whom, device_id_type=MESH,
        )
        sends.append((copy, None))
        copy.start()

    def arrived(name, ref):
        pltpu.make_async_remote_copy(
            ref, ref, send_sem.at[0], recv_sem.at[slots[name]],
            device_id=peer(dc=1), device_id_type=MESH,
        ).wait_recv()

    t_chunk = TH.at[zh, xx(x), c]
    c_chunk = CH.at[zh, x, c]
    loads = [
        pltpu.make_async_copy(bout_t, CB.at[0, Z0], load_sem.at[0]),
        pltpu.make_async_copy(grads.at[:, pl.ds(0, 16)], TB.at[Y0, Z1, 0], load_sem.at[1]),
        pltpu.make_async_copy(grads.at[:, pl.ds(16, 16)], TB.at[Y0, Z1, 1], load_sem.at[2]),
        pltpu.make_async_copy(acts, t_chunk, load_sem.at[3]),
        pltpu.make_async_copy(bin_t, c_chunk, load_sem.at[4]),
    ]
    for load in loads:
        load.start()

    peers = [peer(dc=1)]
    peers += [peer(dx=d) for d in (1, 2, 3)]
    peers += [peer(dzh=d) for d in (1, 3)]
    peers += [peer(dy=d) for d in (1, 3)]
    peers += [peer(dzl=d) for d in (1, 2, 3)]
    barrier = pltpu.get_barrier_semaphore()
    for whom in peers:
        pl.semaphore_signal(barrier, inc=1, device_id=whom, device_id_type=MESH)
    pl.semaphore_wait(barrier, len(peers))
    for load in loads:
        load.wait()

    def th(dzh, dx=0, core=None):
        return TH.at[flip(zh, dzh), xx(flip(x, dx)), c if core is None else core]

    def ch(dzh, dx=0, core=None):
        return CH.at[flip(zh, dzh), flip(x, dx), c if core is None else core]

    def th_half(dzh, half):
        return TH.at[flip(zh, dzh), xx(x), c, half]

    def ch_half(dzh, half):
        return CH.at[flip(zh, dzh), x, c, pl.ds(16 * half, 16)]

    def ro(dy, dzl, piece):
        yy, zz = flip(y, dy), flip(zl, dzl)
        column = 2 * flip(yy, 3 * piece) + zz // 2
        return RO.at[column, yy // 2, :, zz % 2]

    def z_own(kind, chunk):
        for d in (1, 3):
            send((kind, "z", d), chunk(0), peer(dzh=d))

    def x_send(kind, chunk, dzh):
        for d in (1, 3, 2):
            send((kind, "x", dzh, d), chunk(dzh), peer(dx=d))

    def z_relay(kind, chunk, half_of):
        arrived((kind, "z", 1), chunk(1))
        send((kind, "r", 0), half_of(1, 0), peer(dzh=3))
        x_send(kind, chunk, 1)
        arrived((kind, "z", 3), chunk(3))
        send((kind, "r", 1), half_of(3, 1), peer(dzh=1))
        x_send(kind, chunk, 3)

    def z_opposite(kind, chunk, half_of):
        for half in (0, 1):
            arrived((kind, "r", half), half_of(2, half))
        x_send(kind, chunk, 2)

    def core_send(kind, chunk, whole, dzh):
        for d in (1, 3, 2):
            arrived((kind, "x", dzh, d), chunk(dzh, d))
        send((kind, "c", dzh), whole.at[flip(zh, dzh), :, c], peer(dc=1))

    def core_wait(kind, whole, dzh):
        arrived((kind, "c", dzh), whole.at[flip(zh, dzh), :, flip(c, 1)])

    send("Cz", CB.at[0, Z0], peer(dzl=1))
    send("Tz", TB.at[Y0, Z1], peer(dzl=2))
    send_to("Cy", CB.at[0, Z0], CB.at[1, Z0], peer(dy=3))
    send("Ty", TB.at[Y0, Z1], peer(dy=1))
    z_own("T", th)
    x_send("T", th, 0)
    arrived("Cz", CB.at[0, flip(Z0, 1)])
    send_to("Cy2", CB.at[0, flip(Z0, 1)], CB.at[1, flip(Z0, 1)], peer(dy=3))
    arrived("Tz", TB.at[Y0, flip(Z1, 1)])
    send("Ty2", TB.at[Y0, flip(Z1, 1)], peer(dy=1))
    z_relay("T", th, th_half)
    x_send("C", ch, 0)

    arrived("Ty", TB.at[flip(Y0, 1), Z1])
    arrived("Ty2", TB.at[flip(Y0, 1), flip(Z1, 1)])
    arrived("Cy", CB.at[1, Z0])
    arrived("Cy2", CB.at[1, flip(Z0, 1)])
    tokens = TB[...].reshape(256, 1024)
    for piece in (0, 1):
        rotated = nt_dot(tokens, CB[piece].reshape(128, 1024)).astype(bf16)
        ro(0, 0, piece)[...] = rotated.reshape(2, 128, 128)

    def y_send(dzl):
        for piece in (0, 1):
            for d in (1, 3):
                send(("Ry", dzl, piece, d), ro(0, dzl, piece), peer(dy=d))

    def y_relay(dzl):
        arrived(("Ry", dzl, 0, 1), ro(1, dzl, 0))
        send(("Rr", dzl, 0), ro(1, dzl, 0), peer(dy=3))
        arrived(("Ry", dzl, 1, 3), ro(3, dzl, 1))
        send(("Rr", dzl, 1), ro(3, dzl, 1), peer(dy=1))

    for piece in (0, 1):
        send(("Rz", 1, piece), ro(0, 0, piece), peer(dzl=1))
        send(("Rz", 3, piece), ro(0, 0, piece), peer(dzl=3), is_mid)
    y_send(0)
    z_opposite("T", th, th_half)
    z_own("C", ch)
    for piece in (0, 1):
        arrived(("Rz", 1, piece), ro(0, 1, piece))
        send(("Rz", 2, piece), ro(0, 1, piece), peer(dzl=3), is_mid)
    y_send(1)
    y_relay(0)
    for piece in (0, 1):
        arrived(("Rz", 3, piece), ro(0, 3, piece))
        send(("Rz", 2, piece), ro(0, 3, piece), peer(dzl=1), is_mid)
    for piece in (0, 1):
        arrived(("Rz", 2, piece), ro(0, 2, piece))
        send(("Rz", 3, piece), ro(0, 2, piece), peer(dzl=1), is_mid)
    y_send(3)
    y_send(2)
    y_relay(1)
    z_relay("C", ch, ch_half)
    for dzh in (0, 1, 3, 2):
        core_send("T", th, TH, dzh)
    y_relay(3)
    y_relay(2)
    z_opposite("C", ch, ch_half)
    for dzh in (0, 1, 3):
        core_send("C", ch, CH, dzh)
    for dzh in (0, 1, 3, 2):
        core_wait("T", TH, dzh)

    def rotate_plane(dzh):
        plane = flip(zh, dzh)
        columns = CH[plane].reshape(256, 1024)

        @pl.loop(0, 4)
        def _(block):
            rotated = nt_dot(columns, TH[block].reshape(256, 1024)).astype(bf16)
            RT[block] = rotated
            ST[block] = square(rotated)

    def finish_plane(dzh):
        plane = flip(zh, dzh)

        @pl.loop(0, 4)
        def _(block):
            left = jnp.concatenate([RT[i] for i in range(4)], axis=1)
            left_sq = jnp.concatenate([ST[i] for i in range(4)], axis=1)

            def right(ref):
                return jnp.concatenate(
                    [ref[2 * block + i].reshape(1024, 128) for i in (0, 1)], axis=1
                )

            grad = jnp.dot(left, right(RO), preferred_element_type=f32)
            fisher = jnp.dot(left_sq, right(SO), preferred_element_type=f32)
            rows = pl.ds(pl.multiple_of(plane * 256, 256), 256)
            lanes = pl.ds(pl.multiple_of(block * 256, 256), 256)
            out[rows, lanes] = (grad / (fisher + damping)).astype(bf16)

    core_wait("C", CH, 0)
    rotate_plane(0)
    for dzl in (0, 1, 3, 2):
        arrived(("Ry", dzl, 0, 3), ro(3, dzl, 0))
        arrived(("Ry", dzl, 1, 1), ro(1, dzl, 1))
        arrived(("Rr", dzl, 0), ro(2, dzl, 0))
        arrived(("Rr", dzl, 1), ro(2, dzl, 1))

    @pl.loop(0, 8)
    def _(column):
        SO[column] = square(RO[column])

    finish_plane(0)
    for dzh in (1, 3):
        core_wait("C", CH, dzh)
        rotate_plane(dzh)
        finish_plane(dzh)
    core_send("C", ch, CH, 2)
    core_wait("C", CH, 2)
    rotate_plane(2)
    finish_plane(2)
    for copy, when in sends:
        if when is None:
            copy.wait_send()
        else:
            pl.when(when)(copy.wait_send)


def on_device(activations, out_grads, basis_in, basis_out):
    return pl.pallas_call(
        kernel,
        out_shape=jax.ShapeDtypeStruct((1024, 1024), bf16),
        in_specs=[pl.BlockSpec(memory_space=pl.ANY)] * 4,
        out_specs=pl.BlockSpec(memory_space=pltpu.VMEM),
        scratch_shapes=[
            pltpu.VMEM((2, 2, 2, 2, 16, 1024), bf16),
            pltpu.VMEM((2, 2, 64, 1024), bf16),
            pltpu.VMEM((8, 2, 2, 2, 128, 128), bf16),
            pltpu.VMEM((8, 2, 2, 2, 128, 128), bf16),
            pltpu.VMEM((4, 4, 2, 2, 16, 1024), bf16),
            pltpu.VMEM((4, 4, 2, 32, 1024), bf16),
            pltpu.VMEM((4, 256, 256), bf16),
            pltpu.VMEM((4, 256, 256), bf16),
            pltpu.SemaphoreType.DMA((5,)),
            pltpu.SemaphoreType.DMA((128,)),
            pltpu.SemaphoreType.DMA((96,)),
        ],
        compiler_params=pltpu.CompilerParams(
            collective_id=0, has_side_effects=True, vmem_limit_bytes=48 * 2**20
        ),
        name="fused",
    )(activations, out_grads, basis_in.T, basis_out.T)


def solution(mesh):
    return jax.shard_map(
        on_device,
        mesh=mesh,
        in_specs=(P(None, "hid", "inb"), P(None, "inb", "hid"), P("inb", "hid"), P("hid", "inb")),
        out_specs=P("inb", "hid"),
        check_vma=False,
    )
```

time: 510 us -> 79.2 us (0.16); the launches traced: 500 us -> 78.6 us
  waiting for transfers between devices: 459 us -> 0 us
  Pallas kernels: 0 us -> 73.7 us
  matrix products: 24.8 us -> 0 us
  between operations: 13.5 us -> 0.01 us
    all_gather x6 -> x0, waiting for transfers between devices: 457 us -> none  [the longest x2 148 us: on_device(): lax.all_gather(grads_rot[lower_mb:upper_mb], 'inb', axis=1, tiled=True)]
    pallas_call x0 -> x1, Pallas kernels: none -> 73.7 us  [on_device(): pl.pallas_call(kernel, out_shape=jax.ShapeDtypeStruct((1024, 1024), bf16)...]
    dot_general x7 -> x0, matrix products: 24.8 us -> none  [the longest x4 16 us: contract_tokens(): lax.dot_general(left_side, right_side, (((0, 1), (0, 1)), ((), ())), pref...]
  transfers between devices with their start and end apart: 6 -> 0, of which waited for: 6 -> 0; matrix products, arithmetic and copies ran while one was open for 4% -> 0% of each run, Pallas kernels for 0% -> 0%
where the time goes in v1:
time: 79.2 us; the launch traced here: 78.6 us
  Pallas kernels  73.7 us (93%)
  local copies, waits for them, and re-layouts  4.81 us (6%)
    pallas_call x1, Pallas kernels, on_device(): pl.pallas_call(kernel, out_shape=jax.ShapeDtypeStruct((1024, 1024), bf16)...  73.7 us
    unnamed x9, local copies, waits for them, and re-layouts  4.81 us

profile of v1, /device:TPU:1, one launch (start us, length us, event | category | flops | bytes accessed | tf_op | source)
XLA Modules:
  0.0 78.6 jit_solution(4304613478251402429)
XLA Ops:
  0.0 0.0 copy-start
  0.0 0.9 %copy-done = bf16[2,32,1024]{2,1,0:T(8,128)(2,1)S(1)} copy-done((bf16[2,32,1024]{2,1,0:T(8,128)(2,1)S(1)}, bf16[2,32,1024]{2,1,0:T(8,128)(2,1)}, u32[]{:S(2)}) %copy-start) | copy-done | bytes 131096
  0.9 0.0 copy-start.1
  0.9 0.9 %copy-done.1 = bf16[1024,64]{0,1:T(8,128)(2,1)S(1)} copy-done((bf16[1024,64]{0,1:T(8,128)(2,1)S(1)}, bf16[1024,64]{0,1:T(8,128)(2,1)}, u32[]{:S(2)}) %copy-start.1) | copy-done | bytes 131096
  1.8 0.0 copy-start.2
  1.8 0.8 %copy-done.2 = bf16[2,16,1024]{2,1,0:T(8,128)(2,1)S(1)} copy-done((bf16[2,16,1024]{2,1,0:T(8,128)(2,1)S(1)}, bf16[2,16,1024]{2,1,0:T(8,128)(2,1)}, u32[]{:S(2)}) %copy-start.2) | copy-done | bytes 65560
  2.6 0.0 copy-start.3
  2.7 0.8 %copy-done.3 = bf16[1024,32]{0,1:T(8,128)(2,1)S(1)} copy-done((bf16[1024,32]{0,1:T(8,128)(2,1)S(1)}, bf16[1024,32]{0,1:T(8,128)(2,1)}, u32[]{:S(2)}) %copy-start.3) | copy-done | bytes 65560
  3.5 73.7 %fused.1 = bf16[1024,1024]{1,0:T(8,128)(2,1)S(1)} custom-call(bf16[2,16,1024]{2,1,0:T(8,128)(2,1)S(1)} %copy-done.2, bf16[2,32,1024]{2,1,0:T(8,128)(2,1)S(1)} %copy-done, bf16[32,1024]{1,0:T(8,128)(2,1)S(1)} %bitcast.3, bf16[64,1024]{1,0:T(8,128)(2,1)S(1)} %bitcast.2), custom_call_target="tpu_custom_call" | custom-call | tf_op jit(solution)/shard_map/fused/pallas_call | solution.py:281
  77.2 1.3 %copy.6 = bf16[1024,1024]{1,0:T(8,128)(2,1)} copy(bf16[1024,1024]{1,0:T(8,128)(2,1)S(1)} %fused.1) | data formatting | bytes 4194304
Async XLA Ops:
  0.0 0.9 %copy-start = (bf16[2,32,1024]{2,1,0:T(8,128)(2,1)S(1)}, bf16[2,32,1024]{2,1,0:T(8,128)(2,1)}, u32[]{:S(2)}) copy-start(bf16[2,32,1024]{2,1,0:T(8,128)(2,1)} %grads.1) | copy-start | bytes 393220
  0.9 0.9 %copy-start.1 = (bf16[1024,64]{0,1:T(8,128)(2,1)S(1)}, bf16[1024,64]{0,1:T(8,128)(2,1)}, u32[]{:S(2)}) copy-start(bf16[1024,64]{0,1:T(8,128)(2,1)} %param.7) | copy-start | bytes 393220
  1.8 0.8 %copy-start.2 = (bf16[2,16,1024]{2,1,0:T(8,128)(2,1)S(1)}, bf16[2,16,1024]{2,1,0:T(8,128)(2,1)}, u32[]{:S(2)}) copy-start(bf16[2,16,1024]{2,1,0:T(8,128)(2,1)} %acts.1) | copy-start | bytes 196612
  2.6 0.8 %copy-start.3 = (bf16[1024,32]{0,1:T(8,128)(2,1)S(1)}, bf16[1024,32]{0,1:T(8,128)(2,1)}, u32[]{:S(2)}) copy-start(bf16[1024,32]{0,1:T(8,128)(2,1)} %param.6) | copy-start | bytes 196612

commit v2 on v0

v2 whole, which is shorter than its diff:
```python
import functools

import jax
import jax.numpy as jnp
from jax import lax
from jax.experimental import pallas as pl
from jax.experimental.pallas import tpu as pltpu
from jax.sharding import PartitionSpec as P

damping = 0.1
MESH = pl.DeviceIdType.MESH
bf16 = jnp.bfloat16
f32 = jnp.float32


class Names:
    def __init__(self):
        self.slots = {}

    def __getitem__(self, name):
        return self.slots.setdefault(name, len(self.slots))


def square(values):
    wide = values.astype(f32)
    return (wide * wide).astype(bf16)


def nt_dot(left, right):
    return lax.dot_general(
        left, right, (((1,), (1,)), ((), ())), preferred_element_type=f32
    )


def kernel(
    acts, grads, bin_t, bout_t, out,
    TB, CB, RO, SO, TH, CH, RT, ST, load_sem, send_sem, recv_sem,
):
    inb = lax.axis_index("inb")
    hid = lax.axis_index("hid")
    y, zl = inb // 4, inb % 4
    zh, x, c = hid // 8, (hid // 2) % 4, hid % 2

    is_mid = (zl == 1) | (zl == 2)

    def flip(value, mask):
        for bit in (1, 2):
            if mask & bit:
                value = value + bit - 2 * bit * ((value // bit) % 2)
        return value

    def peer(dy=0, dzl=0, dzh=0, dx=0, dc=0):
        return (
            flip(y, dy) * 4 + flip(zl, dzl),
            flip(zh, dzh) * 8 + flip(x, dx) * 2 + flip(c, dc),
        )

    slots, sends = Names(), []

    def send(name, ref, whom, target=None, when=None):
        copy = pltpu.make_async_remote_copy(
            ref, ref if target is None else target,
            send_sem.at[len(sends)], recv_sem.at[slots[name]],
            device_id=whom, device_id_type=MESH,
        )
        sends.append((copy, when))
        if when is None:
            copy.start()
        else:
            pl.when(when)(copy.start)

    def arrived(name, ref):
        pltpu.make_async_remote_copy(
            ref, ref, send_sem.at[0], recv_sem.at[slots[name]],
            device_id=peer(dc=1), device_id_type=MESH,
        ).wait_recv()

    def tb(dy, dzl, half):
        return TB.at[flip(zl, dzl) // 2, flip(y, dy) % 2, half]

    def cb(other, dzl, half):
        return CB.at[other, flip(zl, dzl) % 2, pl.ds(32 * half, 32)]

    def th(dzh, dx, half):
        return TH.at[flip(zh, dzh) % 2, flip(x, dx) % 2, c, half]

    def ch(other, dx, half):
        return CH.at[other, flip(x, dx) // 2, pl.ds(16 * half, 16)]

    def ro(dy, dzl, piece):
        yy, zz = flip(y, dy), flip(zl, dzl)
        return RO.at[2 * flip(yy, 3 * piece) + zz // 2, yy // 2, :, :, zz % 2]

    def rt(dzh, dx, piece):
        zz, ww = flip(zh, dzh), flip(x, dx)
        return RT.at[
            2 * (zz // 2) + ww // 2,
            flip(zz, 3 * piece),
            pl.ds(2 * ((ww // 2 + ww) % 2), 2),
            c,
        ]

    def rt_half(dzh, piece, group, dc=0):
        zz = flip(zh, dzh)
        return RT.at[2 * (zz // 2) + group, flip(zz, 3 * piece), :, flip(c, dc)]

    loads = [
        pltpu.make_async_copy(bout_t, CB.at[0, zl % 2], load_sem.at[0]),
        pltpu.make_async_copy(grads.at[:, pl.ds(0, 16)], tb(0, 0, 0), load_sem.at[1]),
        pltpu.make_async_copy(grads.at[:, pl.ds(16, 16)], tb(0, 0, 1), load_sem.at[2]),
        pltpu.make_async_copy(acts, TH.at[zh % 2, x % 2, c], load_sem.at[3]),
        pltpu.make_async_copy(bin_t, CH.at[0, x // 2], load_sem.at[4]),
    ]
    for load in loads:
        load.start()
    peers = [peer(dc=1)]
    peers += [peer(dx=d) for d in (1, 2, 3)]
    peers += [peer(dzh=d) for d in (1, 3)]
    peers += [peer(dy=d) for d in (1, 2, 3)]
    peers += [peer(dzl=d) for d in (1, 2, 3)]
    barrier = pltpu.get_barrier_semaphore()
    for whom in peers:
        pl.semaphore_signal(barrier, inc=1, device_id=whom, device_id_type=MESH)
    pl.semaphore_wait(barrier, len(peers))
    for load in loads:
        load.wait()

    for half in (0, 1):
        send(("Cz", half), cb(0, 0, half), peer(dzl=1))
        send(("Tz", half), tb(0, 0, half), peer(dzl=2))
    for half in (0, 1):
        send(("Cy", half), cb(0, 0, half), peer(dy=3), cb(1, 0, half))
        send(("Ty", half), tb(0, 0, half), peer(dy=1))
    for half in (0, 1):
        send(("tx", half), th(0, 0, half), peer(dx=1))
        send(("cx", half), ch(0, 0, half), peer(dx=3))
    for half in (0, 1):
        arrived(("Cz", half), cb(0, 1, half))
        send(("Cy2", half), cb(0, 1, half), peer(dy=3), cb(1, 1, half))
        arrived(("Tz", half), tb(0, 2, half))
        send(("Ty2", half), tb(0, 2, half), peer(dy=1))
    for half in (0, 1):
        send(("tz", half), th(0, 0, half), peer(dzh=1))
        send(("cz", half), ch(0, 0, half), peer(dzh=3), ch(1, 0, half))
    for half in (0, 1):
        arrived(("Ty", half), tb(1, 0, half))
        arrived(("Cy", half), cb(1, 0, half))
        arrived(("Ty2", half), tb(1, 2, half))
        arrived(("Cy2", half), cb(1, 1, half))

    def y_send(dzl):
        for piece, d in ((0, 3), (1, 3), (0, 1), (1, 1)):
            send(("Ry", dzl, piece, d), ro(0, dzl, piece), peer(dy=d))

    def y_direct(dzl):
        y_send(dzl)
        for piece in (0, 1):
            send(("Rr", dzl, piece), ro(0, dzl, piece), peer(dy=2))

    def y_relay(dzl):
        arrived(("Ry", dzl, 0, 1), ro(1, dzl, 0))
        send(("Rr", dzl, 0), ro(1, dzl, 0), peer(dy=3))
        arrived(("Ry", dzl, 1, 3), ro(3, dzl, 1))
        send(("Rr", dzl, 1), ro(3, dzl, 1), peer(dy=1))

    def z_wait(dzl):
        for piece in (0, 1):
            arrived(("Rz", dzl, piece), ro(0, dzl, piece))

    def x_send(dzh, piece):
        for d in (2, 1, 3):
            send(("rx", dzh, d, piece), rt(dzh, 0, piece), peer(dx=d))

    def core_send(dzh, *pieces):
        for piece in pieces:
            for d in (1, 3, 2):
                arrived(("rx", dzh, d, piece), rt(dzh, d, piece))
            for group in (0, 1):
                send(("rc", dzh, piece, group), rt_half(dzh, piece, group), peer(dc=1))

    def core_wait(dzh, *pieces):
        for piece in pieces:
            for group in (0, 1):
                arrived(("rc", dzh, piece, group), rt_half(dzh, piece, group, 1))

    tokens = TB[...].reshape(256, 1024)
    for piece in (0, 1):
        rotated = nt_dot(tokens, CB[piece].reshape(128, 1024)).astype(bf16)
        ro(0, 0, piece)[...] = rotated.reshape(2, 2, 64, 128)
    for d in (2, 1):
        for piece in (0, 1):
            send(("Rz", d, piece), ro(0, 0, piece), peer(dzl=d))
    for piece in (0, 1):
        send(("Rz", 3, piece), ro(0, 0, piece), peer(dzl=3), when=is_mid)
    y_send(0)
    for half in (0, 1):
        arrived(("tz", half), th(1, 0, half))
        send(("tx2", half), th(1, 0, half), peer(dx=1))
        arrived(("cz", half), ch(1, 0, half))
        send(("cx2", half), ch(1, 0, half), peer(dx=3))
    for half in (0, 1):
        arrived(("tx", half), th(0, 1, half))
        arrived(("cx", half), ch(0, 3, half))
    send("tc", TH.at[zh % 2, :, c], peer(dc=1))
    for half in (0, 1):
        arrived(("tx2", half), th(1, 1, half))
    send("tc2", TH.at[1 - zh % 2, :, c], peer(dc=1))
    for half in (0, 1):
        arrived(("cx2", half), ch(1, 3, half))
    z_wait(2)
    for piece in (0, 1):
        send(("Rz", 3, piece), ro(0, 2, piece), peer(dzl=1), when=is_mid)
    y_send(2)
    arrived("tc", TH.at[zh % 2, :, 1 - c])
    arrived("tc2", TH.at[1 - zh % 2, :, 1 - c])
    rotated = nt_dot(CH[...].reshape(128, 1024), TH[...].reshape(256, 1024)).astype(bf16)
    for piece in (0, 1):
        rt(0, 0, piece)[...] = rotated[64 * piece : 64 * piece + 64].reshape(2, 32, 256)
    for d, piece in ((1, 0), (3, 1), (1, 1), (3, 0)):
        send(("rz", d, piece), rt(0, 0, piece), peer(dzh=d))
    x_send(0, 0)
    x_send(0, 1)
    z_wait(1)
    y_send(1)
    y_relay(0)
    y_relay(2)
    y_relay(1)
    z_wait(3)
    y_direct(3)
    arrived(("rz", 1, 0), rt(1, 0, 0))
    send(("rr", 0), rt(1, 0, 0), peer(dzh=3))
    arrived(("rz", 3, 1), rt(3, 0, 1))
    send(("rr", 1), rt(3, 0, 1), peer(dzh=1))
    x_send(3, 1)
    arrived(("rz", 3, 0), rt(3, 0, 0))
    x_send(3, 0)
    x_send(1, 0)
    arrived(("rz", 1, 1), rt(1, 0, 1))
    x_send(1, 1)
    def square_rows(dzh):
        row = flip(zh, dzh)

        @pl.loop(0, 4)
        def _(group):
            ST[group, row] = square(RT[group, row])

    def square_columns(dy):
        first = 2 * flip(y, dy)

        @pl.loop(0, 2)
        def _(i):
            SO[first + i] = square(RO[first + i])

    def finish(dzh, dy):
        row, column = flip(zh, dzh), flip(y, dy)

        def left(ref):
            return jnp.concatenate(
                [ref[group, row].reshape(256, 256) for group in range(4)], axis=1
            )

        def right(ref):
            return jnp.concatenate(
                [ref[2 * column + i].reshape(1024, 128) for i in (0, 1)], axis=1
            )

        grad = jnp.dot(left(RT), right(RO), preferred_element_type=f32)
        fisher = jnp.dot(left(ST), right(SO), preferred_element_type=f32)
        result = (grad / (fisher + damping)).astype(bf16)
        lanes = pl.ds(pl.multiple_of(column * 256, 256), 256)
        for place, part in enumerate((0, 3, 1, 2)):
            rows = pl.ds(pl.multiple_of(row * 256 + 64 * part, 64), 64)
            out[rows, lanes] = result[64 * place : 64 * place + 64]

    core_send(0, 0, 1)
    for piece in (1, 0):
        arrived(("rr", piece), rt(2, 0, piece))
        x_send(2, piece)
    core_send(3, 1, 0)
    for dzl in (0, 1, 2, 3):
        arrived(("Ry", dzl, 0, 3), ro(3, dzl, 0))
    arrived(("Ry", 3, 1, 3), ro(3, 3, 1))
    square_columns(0)
    square_columns(3)
    for dzh in (0, 3):
        core_wait(dzh, 0, 1)
    for dzh in (0, 3):
        square_rows(dzh)
    finish(0, 0)
    finish(3, 0)
    core_send(1, 0, 1)
    finish(0, 3)
    finish(3, 3)
    core_send(2, 1)
    arrived(("Ry", 3, 0, 1), ro(1, 3, 0))
    for dzl in (0, 1, 2, 3):
        arrived(("Ry", dzl, 1, 1), ro(1, dzl, 1))
        arrived(("Rr", dzl, 0), ro(2, dzl, 0))
        arrived(("Rr", dzl, 1), ro(2, dzl, 1))
    square_columns(1)
    square_columns(2)
    finish(0, 1)
    finish(3, 1)
    core_send(2, 0)
    finish(0, 2)
    finish(3, 2)
    core_wait(1, 0)
    core_wait(2, 1)
    square_rows(1)
    for dy in (0, 3, 1, 2):
        finish(1, dy)
    core_wait(1, 1)
    core_wait(2, 0)
    square_rows(2)
    for dy in (0, 3, 1, 2):
        finish(2, dy)
    for copy, when in sends:
        if when is None:
            copy.wait_send()
        else:
            pl.when(when)(copy.wait_send)


def on_device(activations, out_grads, basis_in, basis_out):
    shards = (activations, out_grads, basis_in.T, basis_out.T)
    return pl.pallas_call(
        kernel,
        out_shape=jax.ShapeDtypeStruct((1024, 1024), bf16),
        in_specs=[pl.BlockSpec(memory_space=pltpu.HBM)] * 4,
        out_specs=pl.BlockSpec(memory_space=pltpu.VMEM),
        scratch_shapes=[
            pltpu.VMEM((2, 2, 2, 2, 16, 1024), bf16),
            pltpu.VMEM((2, 2, 64, 1024), bf16),
            pltpu.VMEM((8, 2, 2, 2, 2, 64, 128), bf16),
            pltpu.VMEM((8, 2, 2, 2, 2, 64, 128), bf16),
            pltpu.VMEM((2, 2, 2, 2, 16, 1024), bf16),
            pltpu.VMEM((2, 2, 32, 1024), bf16),
            pltpu.VMEM((4, 4, 4, 2, 32, 256), bf16),
            pltpu.VMEM((4, 4, 4, 2, 32, 256), bf16),
            pltpu.SemaphoreType.DMA((5,)),
            pltpu.SemaphoreType.DMA((128,)),
            pltpu.SemaphoreType.DMA((112,)),
        ],
        compiler_params=pltpu.CompilerParams(
            collective_id=0, has_side_effects=True, vmem_limit_bytes=48 * 2**20
        ),
        name="fused",
    )(*(pltpu.with_memory_space_constraint(shard, pltpu.HBM) for shard in shards))


def solution(mesh):
    return jax.shard_map(
        on_device,
        mesh=mesh,
        in_specs=(P(None, "hid", "inb"), P(None, "inb", "hid"), P("inb", "hid"), P("hid", "inb")),
        out_specs=P("inb", "hid"),
        check_vma=False,
    )
```

time: 510 us -> 62.4 us (0.12); the launches traced: 500 us -> 61.6 us
  waiting for transfers between devices: 459 us -> 0 us
  Pallas kernels: 0 us -> 60.3 us
  matrix products: 24.8 us -> 0 us
  between operations: 13.5 us -> 0.01 us
    all_gather x6 -> x0, waiting for transfers between devices: 457 us -> none  [the longest x2 148 us: on_device(): lax.all_gather(grads_rot[lower_mb:upper_mb], 'inb', axis=1, tiled=True)]
    pallas_call x0 -> x1, Pallas kernels: none -> 60.3 us  [on_device(): pl.pallas_call(kernel, out_shape=jax.ShapeDtypeStruct((1024, 1024), bf16)...]
    dot_general x7 -> x0, matrix products: 24.8 us -> none  [the longest x4 16 us: contract_tokens(): lax.dot_general(left_side, right_side, (((0, 1), (0, 1)), ((), ())), pref...]
  transfers between devices with their start and end apart: 6 -> 0, of which waited for: 6 -> 0; matrix products, arithmetic and copies ran while one was open for 4% -> 0% of each run, Pallas kernels for 0% -> 0%
where the time goes in v2:
time: 62.4 us; the launch traced here: 61.6 us
  Pallas kernels  60.3 us (97%)
  local copies, waits for them, and re-layouts  1.32 us (2%)
    pallas_call x1, Pallas kernels, on_device(): pl.pallas_call(kernel, out_shape=jax.ShapeDtypeStruct((1024, 1024), bf16)...  60.3 us
    unnamed x1, local copies, waits for them, and re-layouts  1.32 us

profile of v2, /device:TPU:1, one launch (start us, length us, event | category | flops | bytes accessed | tf_op | source)
XLA Modules:
  0.0 61.6 jit_solution(1293780519745912383)
XLA Ops:
  0.0 60.3 %fused.1 = bf16[1024,1024]{1,0:T(8,128)(2,1)S(1)} custom-call(bf16[2,16,1024]{2,1,0:T(8,128)(2,1)} %acts.1, bf16[2,32,1024]{2,1,0:T(8,128)(2,1)} %grads.1, bf16[32,1024]{1,0:T(8,128)(2,1)} %bitcast.3, bf16[64,1024]{1,0:T(8,128)(2,1)} %bitcast.2), custom_call_target="tpu_custom_call" | custom-call | tf_op jit(solution)/shard_map/fused/pallas_call | solution.py:326
  60.3 1.3 %copy.6 = bf16[1024,1024]{1,0:T(8,128)(2,1)} copy(bf16[1024,1024]{1,0:T(8,128)(2,1)S(1)} %fused.1) | data formatting | bytes 4194304

commit v3 on v2

--- a/solution.py
+++ b/solution.py
@@ -139,7 +139,6 @@
         send(("Cy2", half), cb(0, 1, half), peer(dy=3), cb(1, 1, half))
         arrived(("Tz", half), tb(0, 2, half))
         send(("Ty2", half), tb(0, 2, half), peer(dy=1))
-    for half in (0, 1):
         send(("tz", half), th(0, 0, half), peer(dzh=1))
         send(("cz", half), ch(0, 0, half), peer(dzh=3), ch(1, 0, half))
     for half in (0, 1):
@@ -237,12 +236,12 @@
     x_send(1, 0)
     arrived(("rz", 1, 1), rt(1, 0, 1))
     x_send(1, 1)
-    def square_rows(dzh):
+    def square_rows(dzh, core):
         row = flip(zh, dzh)
 
         @pl.loop(0, 4)
         def _(group):
-            ST[group, row] = square(RT[group, row])
+            ST[group, row, :, core] = square(RT[group, row, :, core])
 
     def square_columns(dy):
         first = 2 * flip(y, dy)
@@ -273,10 +272,12 @@
             out[rows, lanes] = result[64 * place : 64 * place + 64]
 
     core_send(0, 0, 1)
+    core_send(3, 1, 0)
     for piece in (1, 0):
         arrived(("rr", piece), rt(2, 0, piece))
         x_send(2, piece)
-    core_send(3, 1, 0)
+    for dzh in (0, 3):
+        square_rows(dzh, c)
     for dzl in (0, 1, 2, 3):
         arrived(("Ry", dzl, 0, 3), ro(3, dzl, 0))
     arrived(("Ry", 3, 1, 3), ro(3, 3, 1))
@@ -285,7 +286,7 @@
     for dzh in (0, 3):
         core_wait(dzh, 0, 1)
     for dzh in (0, 3):
-        square_rows(dzh)
+        square_rows(dzh, 1 - c)
     finish(0, 0)
     finish(3, 0)
     core_send(1, 0, 1)
@@ -306,12 +307,14 @@
     finish(3, 2)
     core_wait(1, 0)
     core_wait(2, 1)
-    square_rows(1)
+    square_rows(1, c)
+    square_rows(1, 1 - c)
     for dy in (0, 3, 1, 2):
         finish(1, dy)
     core_wait(1, 1)
     core_wait(2, 0)
-    square_rows(2)
+    square_rows(2, c)
+    square_rows(2, 1 - c)
     for dy in (0, 3, 1, 2):
         finish(2, dy)
     for copy, when in sends:

time: 62.4 us -> 61.4 us (0.984); the launches traced: 61.6 us -> 61.3 us
  no operation moved by 1% of the time
where the time goes in v3:
time: 61.4 us; the launch traced here: 61.3 us
  Pallas kernels  60 us (98%)
  local copies, waits for them, and re-layouts  1.32 us (2%)
    pallas_call x1, Pallas kernels, on_device(): pl.pallas_call(kernel, out_shape=jax.ShapeDtypeStruct((1024, 1024), bf16)...  60 us
    unnamed x1, local copies, waits for them, and re-layouts  1.32 us

profile of v3, /device:TPU:1, one launch (start us, length us, event | category | flops | bytes accessed | tf_op | source)
XLA Modules:
  0.0 61.3 jit_solution(17569375023977946787)
XLA Ops:
  0.0 60.0 %fused.1 = bf16[1024,1024]{1,0:T(8,128)(2,1)S(1)} custom-call(bf16[2,16,1024]{2,1,0:T(8,128)(2,1)} %acts.1, bf16[2,32,1024]{2,1,0:T(8,128)(2,1)} %grads.1, bf16[32,1024]{1,0:T(8,128)(2,1)} %bitcast.3, bf16[64,1024]{1,0:T(8,128)(2,1)} %bitcast.2), custom_call_target="tpu_custom_call" | custom-call | tf_op jit(solution)/shard_map/fused/pallas_call | solution.py:329
  60.0 1.3 %copy.6 = bf16[1024,1024]{1,0:T(8,128)(2,1)} copy(bf16[1024,1024]{1,0:T(8,128)(2,1)S(1)} %fused.1) | data formatting | bytes 4194304

commit v4 on v3

--- a/solution.py
+++ b/solution.py
@@ -126,8 +126,8 @@
         load.wait()
 
     for half in (0, 1):
+        send(("Tz", half), tb(0, 0, half), peer(dzl=2))
         send(("Cz", half), cb(0, 0, half), peer(dzl=1))
-        send(("Tz", half), tb(0, 0, half), peer(dzl=2))
     for half in (0, 1):
         send(("Cy", half), cb(0, 0, half), peer(dy=3), cb(1, 0, half))
         send(("Ty", half), tb(0, 0, half), peer(dy=1))
@@ -255,7 +255,14 @@
 
         def left(ref):
             return jnp.concatenate(
-                [ref[group, row].reshape(256, 256) for group in range(4)], axis=1
+                [
+                    jnp.concatenate(
+                        [ref[group, row, place].reshape(64, 256) for place in (0, 2, 3, 1)],
+                        axis=0,
+                    )
+                    for group in range(4)
+                ],
+                axis=1,
             )
 
         def right(ref):
@@ -265,11 +272,10 @@
 
         grad = jnp.dot(left(RT), right(RO), preferred_element_type=f32)
         fisher = jnp.dot(left(ST), right(SO), preferred_element_type=f32)
-        result = (grad / (fisher + damping)).astype(bf16)
-        lanes = pl.ds(pl.multiple_of(column * 256, 256), 256)
-        for place, part in enumerate((0, 3, 1, 2)):
-            rows = pl.ds(pl.multiple_of(row * 256 + 64 * part, 64), 64)
-            out[rows, lanes] = result[64 * place : 64 * place + 64]
+        out[
+            pl.ds(pl.multiple_of(row * 256, 256), 256),
+            pl.ds(pl.multiple_of(column * 256, 256), 256),
+        ] = (grad / (fisher + damping)).astype(bf16)
 
     core_send(0, 0, 1)
     core_send(3, 1, 0)

time: 61.4 us -> 61 us (level)
  no operation moved by 1% of the time
where the time goes in v4:
time: 61 us; the launch traced here: 60.9 us
  Pallas kernels  59.6 us (98%)
  local copies, waits for them, and re-layouts  1.32 us (2%)
    pallas_call x1, Pallas kernels, on_device(): pl.pallas_call(kernel, out_shape=jax.ShapeDtypeStruct((1024, 1024), bf16)...  59.6 us
    unnamed x1, local copies, waits for them, and re-layouts  1.32 us

profile of v4, /device:TPU:1, one launch (start us, length us, event | category | flops | bytes accessed | tf_op | source)
XLA Modules:
  0.0 60.9 jit_solution(4774176919682324457)
XLA Ops:
  0.0 59.6 %fused.1 = bf16[1024,1024]{1,0:T(8,128)(2,1)S(1)} custom-call(bf16[2,16,1024]{2,1,0:T(8,128)(2,1)} %acts.1, bf16[2,32,1024]{2,1,0:T(8,128)(2,1)} %grads.1, bf16[32,1024]{1,0:T(8,128)(2,1)} %bitcast.3, bf16[64,1024]{1,0:T(8,128)(2,1)} %bitcast.2), custom_call_target="tpu_custom_call" | custom-call | tf_op jit(solution)/shard_map/fused/pallas_call | solution.py:335
  59.6 1.3 %copy.6 = bf16[1024,1024]{1,0:T(8,128)(2,1)} copy(bf16[1024,1024]{1,0:T(8,128)(2,1)S(1)} %fused.1) | data formatting | bytes 4194304
